TPU v7x, 512 devices: a whole 4x4x16 slice. The times are simulated.
512 devices in a mesh: dp: 4 (over y), expert: 32 (over z, core), tensor: 4 (over x).
Axes of the slice: x: 4, y: 4, z: 16, core: 2. Of those that a mesh axis runs over, the one named last changes fastest.
Arguments:
- tokens: bfloat16 [16384, 2048], P(('dp', 'expert')), may hold values from -6 to 6
- cotangent: bfloat16 [16384, 2048], P(('dp', 'expert')), may hold values from -6 to 6
- expert_ids: int32 [16384, 1], P(('dp', 'expert')), may hold values from 0 to 31; in each aligned block of 128 rows (0 to 127, 128 to 255, ...) at most 8 rows name the same one
- gate_weight: bfloat16 [32, 2048, 1408], P('expert', 'dp', 'tensor'), may hold values from -0.125 to 0.125
- up_weight: bfloat16 [32, 2048, 1408], P('expert', 'dp', 'tensor'), may hold values from -0.125 to 0.125
- down_weight: bfloat16 [32, 2048, 1408], P('expert', 'dp', 'tensor'), may hold values from -0.15625 to 0.15625
Outputs:
- grad_tokens: bfloat16 [16384, 2048], P(('dp', 'expert'), 'tensor')
- grad_gate: bfloat16 [32, 2048, 1408], P('expert', 'dp', 'tensor')
- grad_up: bfloat16 [32, 2048, 1408], P('expert', 'dp', 'tensor')
Inputs may be any that keep to these rules, and one draw needn't show every extreme that they name: `expert_ids`: among the 128 tokens of one block no expert id occurs more than 8 times, and in every draw some block holds some id exactly 8 times.
All inputs are finite; a program needn't handle non-finite values.
Results may differ from a plain program's by a relative error of at most 0.013.
Values may be sent and summed in bfloat16 or wider, within the bound.
A program may use at most 64 MiB of HBM per device.

v0:
```python
import jax
import jax.numpy as jnp
from jax import lax
from jax.sharding import PartitionSpec as P

CAP = 8


def bucket_matrix(expert_ids, expert_count, capacity):
    chosen = expert_ids[:, 0]
    columns = jnp.arange(expert_count, dtype=jnp.int32)
    onehot = (chosen[:, None] == columns[None, :]).astype(jnp.int32)
    earlier = jnp.cumsum(onehot, axis=0) - onehot
    position = jnp.sum(earlier * onehot, axis=1)
    target = chosen * capacity + position
    slot_rows = jnp.arange(expert_count * capacity, dtype=jnp.int32)
    return (slot_rows[:, None] == target[None, :]).astype(jnp.bfloat16)


def on_device(tokens, cotangent, expert_ids, gate_weight, up_weight, down_weight):
    owners = lax.axis_size("expert")
    feature_count = tokens.shape[1]
    local_experts = gate_weight.shape[0]
    expert_count = local_experts * owners
    slot_count = owners * CAP
    placer = bucket_matrix(expert_ids, expert_count, CAP)
    gate_full, up_full, down_full = (
        lax.all_gather(gate_weight, "dp", axis=1, tiled=True),
        lax.all_gather(up_weight, "dp", axis=1, tiled=True),
        lax.all_gather(down_weight, "dp", axis=1, tiled=True),
    )

    def to_buckets(rows):
        packed = jnp.dot(placer, rows, preferred_element_type=jnp.float32).astype(jnp.bfloat16)
        return packed.reshape(owners, local_experts, CAP, rows.shape[1])

    arrived_tokens, arrived_grads = (
        lax.all_to_all(to_buckets(tokens), "expert", split_axis=0, concat_axis=2, tiled=True),
        lax.all_to_all(to_buckets(cotangent), "expert", split_axis=0, concat_axis=2, tiled=True),
    )
    inputs = arrived_tokens.reshape(local_experts, slot_count, feature_count)
    grads_in = arrived_grads.reshape(local_experts, slot_count, feature_count)
    gate_act = jnp.einsum("esd,edf->esf", inputs, gate_full, preferred_element_type=jnp.float32)
    up_act = jnp.einsum("esd,edf->esf", inputs, up_full, preferred_element_type=jnp.float32)
    hidden_grad = jnp.einsum(
        "esd,edf->esf", grads_in, down_full, preferred_element_type=jnp.float32
    )
    sigmoid_gate = jax.nn.sigmoid(gate_act)
    up_grad = (hidden_grad * gate_act * sigmoid_gate).astype(jnp.bfloat16)
    gate_grad = (
        hidden_grad * up_act * sigmoid_gate * (1.0 + gate_act * (1.0 - sigmoid_gate))
    ).astype(jnp.bfloat16)
    partial_value = jnp.einsum(
        "esf,edf->esd", gate_grad, gate_full, preferred_element_type=jnp.float32
    )
    partial_value = partial_value + jnp.einsum(
        "esf,edf->esd", up_grad, up_full, preferred_element_type=jnp.float32
    )
    gate_term = jnp.einsum("esd,esf->edf", inputs, gate_grad, preferred_element_type=jnp.float32)
    up_term = jnp.einsum("esd,esf->edf", inputs, up_grad, preferred_element_type=jnp.float32)
    grad_gate, grad_up = (
        lax.psum_scatter(
            gate_term.astype(jnp.bfloat16), "dp", scatter_dimension=1, tiled=True
        ).astype(jnp.float32),
        lax.psum_scatter(
            up_term.astype(jnp.bfloat16), "dp", scatter_dimension=1, tiled=True
        ).astype(jnp.float32),
    )
    contract = (((0,), (0,)), ((), ()))
    outgoing_back = partial_value.astype(jnp.bfloat16).reshape(
        1, local_experts, slot_count, feature_count
    )
    returned = lax.all_to_all(outgoing_back, "expert", split_axis=2, concat_axis=0, tiled=True)
    flat_rows = returned.reshape(expert_count * CAP, feature_count)
    per_token = lax.dot_general(placer, flat_rows, contract, preferred_element_type=jnp.float32)
    summed = lax.psum_scatter(
        per_token.astype(jnp.bfloat16), "tensor", scatter_dimension=1, tiled=True
    )
    return (summed, grad_gate.astype(jnp.bfloat16), grad_up.astype(jnp.bfloat16))


def solution(mesh):
    placed = (
        P(("dp", "expert"), None),
        P(("dp", "expert"), None),
        P(("dp", "expert"), None),
        P("expert", "dp", "tensor"),
        P("expert", "dp", "tensor"),
        P("expert", "dp", "tensor"),
    )
    return jax.shard_map(
        on_device,
        mesh=mesh,
        in_specs=placed,
        out_specs=(
            P(("dp", "expert"), "tensor"),
            P("expert", "dp", "tensor"),
            P("expert", "dp", "tensor"),
        ),
        check_vma=False,
    )
```

profile of v0, /device:TPU:8, one launch (start us, length us, event | category | flops | bytes accessed | tf_op | source)
XLA Modules:
  0.0 280.9 jit_solution(13116984333326666507)
XLA Ops:
  7.2 0.8 fusion.37
  8.2 0.8 select_reduce_fusion
  9.7 1.4 fusion.5
  11.1 15.6 %all-to-all-start.1 = ((bf16[32,1,8,2048]{3,2,1,0:T(8,128)(2,1)}), bf16[32,1,8,2048]{3,2,1,0:T(8,128)(2,1)S(1)}, u32[]{:S(2)}, u32[]{:S(2)}) async-start(bf16[32,1,8,2048]{3,2,1,0:T(8,128)(2,1)} %fusion.5), calls=%async_computation.1 | async-start | bytes 2097152 | tf_op jit(solution)/shard_map/all_to_all | solution.py:38
  27.4 1.4 fusion.4
  28.8 53.8 %all-to-all-done.1 = bf16[32,1,8,2048]{3,2,1,0:T(8,128)(2,1)S(1)} async-done(((bf16[32,1,8,2048]{3,2,1,0:T(8,128)(2,1)}), bf16[32,1,8,2048]{3,2,1,0:T(8,128)(2,1)S(1)}, u32[]{:S(2)}, u32[]{:S(2)}) %all-to-all-start.1) | async-done | bytes 1048608 | tf_op jit(solution)/shard_map/all_to_all | solution.py:38
  82.7 3.9 %all-to-all-start = ((bf16[32,1,8,2048]{3,2,1,0:T(8,128)(2,1)}), bf16[32,1,8,2048]{3,2,1,0:T(8,128)(2,1)S(1)}, u32[]{:S(2)}, u32[]{:S(2)}) async-start(bf16[32,1,8,2048]{3,2,1,0:T(8,128)(2,1)} %fusion.4), calls=%async_computation | async-start | bytes 2097152 | tf_op jit(solution)/shard_map/all_to_all | solution.py:39
  88.3 1.9 fusion.8
  90.3 32.8 %all-gather.4.cloned.1.call-done = bf16[1,2048,352]{1,2,0:T(8,128)(2,1)} async-done(((bf16[1,512,352]{1,2,0:T(8,128)(2,1)}), bf16[1,2048,352]{1,2,0:T(8,128)(2,1)}) %all-gather.4.cloned.1.call-update) | async-done | bytes 1441808 | tf_op jit(solution)/shard_map/all_gather | solution.py:30
  123.0 20.1 %all-to-all-done = bf16[32,1,8,2048]{3,2,1,0:T(8,128)(2,1)S(1)} async-done(((bf16[32,1,8,2048]{3,2,1,0:T(8,128)(2,1)}), bf16[32,1,8,2048]{3,2,1,0:T(8,128)(2,1)S(1)}, u32[]{:S(2)}, u32[]{:S(2)}) %all-to-all-start) | async-done | bytes 1048608 | tf_op jit(solution)/shard_map/all_to_all | solution.py:39
  143.1 2.7 multiply_convert_fusion
  145.9 13.1 %all-gather.6.cloned.1.call-done = bf16[1,2048,352]{1,2,0:T(8,128)(2,1)} async-done(((bf16[1,512,352]{1,2,0:T(8,128)(2,1)}), bf16[1,2048,352]{1,2,0:T(8,128)(2,1)}) %all-gather.6.cloned.1.call-update) | async-done | bytes 1441808 | tf_op jit(solution)/shard_map/all_gather | solution.py:29
  158.9 2.0 fusion.24
  160.9 1.7 fusion.1
  164.0 0.7 fusion.3
  164.7 2.9 %copy.21 = bf16[1,1,256,2048]{3,1,0,2:T(2,128)(2,1)} copy(bf16[1,1,256,2048]{3,2,1,0:T(8,128)(2,1)S(1)} %fusion.3) | data formatting | bytes 2097152 | tf_op jit(solution)/shard_map/reshape | solution.py:70
  168.2 8.0 %reduce = bf16[256,2048]{1,0:T(8,128)(2,1)S(1)} reduce(bf16[256,1,1,2048]{3,2,1,0:T(2,128)(2,1)} %bitcast.66, bf16[]{:T(256)} %broadcast.19), dimensions={1,2}, to_apply=%bitcast.65.reduce_sub_computation | reduce | bytes 2097154
  176.2 1.9 reshape.108
  178.1 12.6 %all-to-all-start.2 = ((bf16[32,2,8192]{2,1,0:T(2,128)(2,1)}), bf16[32,2,8192]{2,1,0:T(2,128)(2,1)S(1)}, u32[]{:S(2)}, u32[]{:S(2)}) async-start(bf16[32,2,8192]{2,1,0:T(2,128)(2,1)} %reshape.108), calls=%async_computation.2 | async-start | bytes 2097152 | tf_op jit(solution)/shard_map/all_to_all | solution.py:73
  190.8 1.7 fusion.2
  192.5 54.2 %all-to-all-done.2 = bf16[32,2,8192]{2,1,0:T(2,128)(2,1)S(1)} async-done(((bf16[32,2,8192]{2,1,0:T(2,128)(2,1)}), bf16[32,2,8192]{2,1,0:T(2,128)(2,1)S(1)}, u32[]{:S(2)}, u32[]{:S(2)}) %all-to-all-start.2) | async-done | bytes 1048608 | tf_op jit(solution)/shard_map/all_to_all | solution.py:73
  246.7 3.5 %reshape.109 = bf16[256,1,1,2048]{3,2,1,0:T(2,128)(2,1)} reshape(bf16[32,2,8192]{2,1,0:T(2,128)(2,1)S(1)} %all-to-all-done.2) | data formatting | bytes 2097152
  250.1 3.1 %convolution_convert_fusion.4 = bf16[128,2048]{1,0:T(8,128)(2,1)} fusion(bf16[1,1,256,2048]{3,1,0,2:T(2,128)(2,1)} %bitcast.67, s32[128]{0:T(128)S(1)} %multiply_add_fusion), kind=kOutput, calls=%fused_computation.11 | convolution fusion | flops 134512640 | bytes 1573376 | tf_op jit(solution)/shard_map/dot_general | solution.py:75
  253.4 20.7 %reduce-scatter.4.cloned.1.call-done = bf16[128,512]{1,0:T(8,128)(2,1)} async-done(((bf16[128,2048]{1,0:T(8,128)(2,1)}), bf16[128,512]{1,0:T(8,128)(2,1)}) %reduce-scatter.4.cloned.1.call-update) | async-done | bytes 131088 | tf_op jit(solution)/shard_map/reduce_scatter | solution.py:76
  (27 shorter events, 5.3 us)
Async XLA Ops:
  7.2 2.5 copy-start
  11.1 16.4 %copy-start.3 = (bf16[128,2048]{1,0:T(8,128)(2,1)S(1)}, bf16[128,2048]{1,0:T(8,128)(2,1)}, u32[]{:S(2)}) copy-start(bf16[128,2048]{1,0:T(8,128)(2,1)} %param.7) | copy-start | bytes 1572868
  11.1 71.6 %all-to-all-start.1 = ((bf16[32,1,8,2048]{3,2,1,0:T(8,128)(2,1)}), bf16[32,1,8,2048]{3,2,1,0:T(8,128)(2,1)S(1)}, u32[]{:S(2)}, u32[]{:S(2)}) async-start(bf16[32,1,8,2048]{3,2,1,0:T(8,128)(2,1)} %fusion.5), calls=%async_computation.1 | async-start | bytes 2097152 | tf_op jit(solution)/shard_map/all_to_all | solution.py:38
  26.7 61.7 %all-gather.8.cloned.1.call-start = ((), (), s32[]{:S(2)}) async-start(), calls=%async_computation.8 | async-start | bytes 1802240 | tf_op jit(solution)/shard_map/all_gather | solution.py:28
  82.7 60.4 %all-to-all-start = ((bf16[32,1,8,2048]{3,2,1,0:T(8,128)(2,1)}), bf16[32,1,8,2048]{3,2,1,0:T(8,128)(2,1)S(1)}, u32[]{:S(2)}, u32[]{:S(2)}) async-start(bf16[32,1,8,2048]{3,2,1,0:T(8,128)(2,1)} %fusion.4), calls=%async_computation | async-start | bytes 2097152 | tf_op jit(solution)/shard_map/all_to_all | solution.py:39
  86.6 36.4 %all-gather.4.cloned.1.call-start = ((), (), s32[]{:S(2)}) async-start(), calls=%async_computation.6 | async-start | bytes 1802240 | tf_op jit(solution)/shard_map/all_gather | solution.py:30
  87.4 71.6 %all-gather.6.cloned.1.call-start = ((), (), s32[]{:S(2)}) async-start(), calls=%async_computation.7 | async-start | bytes 1802240 | tf_op jit(solution)/shard_map/all_gather | solution.py:29
  88.1 165.2 %reduce-scatter.6.cloned.1.call-start = ((), (), s32[]{:S(2)}) async-start(), calls=%async_computation.10 | async-start | bytes 1802240 | tf_op jit(solution)/shard_map/reduce_scatter | solution.py:62
  160.9 1.7 copy-start.1
  162.6 1.4 copy-start.2
  178.1 68.6 %all-to-all-start.2 = ((bf16[32,2,8192]{2,1,0:T(2,128)(2,1)}), bf16[32,2,8192]{2,1,0:T(2,128)(2,1)S(1)}, u32[]{:S(2)}, u32[]{:S(2)}) async-start(bf16[32,2,8192]{2,1,0:T(2,128)(2,1)} %reshape.108), calls=%async_computation.2 | async-start | bytes 2097152 | tf_op jit(solution)/shard_map/all_to_all | solution.py:73
  190.7 62.6 %reduce-scatter.8.cloned.1.call-start = ((), (), s32[]{:S(2)}) async-start(), calls=%async_computation.11 | async-start | bytes 1802240 | tf_op jit(solution)/shard_map/reduce_scatter | solution.py:65
  192.4 81.7 %reduce-scatter.4.cloned.1.call-start = ((), (), s32[]{:S(2)}) async-start(), calls=%async_computation.9 | async-start | bytes 655360 | tf_op jit(solution)/shard_map/reduce_scatter | solution.py:76
Sparse Core Ops, SparseCore 0:
  29.6 33.4 all-gather.7
  89.5 33.4 all-gather.3
  125.1 33.7 all-gather.5
  162.8 32.7 reduce-scatter.5
  198.8 32.4 reduce-scatter.7
  253.4 20.6 reduce-scatter.3
where the time goes:
time: 282 us; the launch traced here: 281 us
  waiting for transfers between devices  197 us (70%)
  starting transfers between devices  32.5 us (12%)
  matrix products  17.4 us (6%)
  between operations  14.2 us (5%)
  other arithmetic  10.5 us (4%)
  local copies, waits for them, and re-layouts  9.44 us (3%)
    all_to_all x1, waiting for transfers between devices, on_device(): lax.all_to_all(outgoing_back, 'expert', split_axis=2, concat_axis=0, tile...  54.2 us
    all_to_all x1, waiting for transfers between devices, on_device(): lax.all_to_all(to_buckets(tokens), 'expert', split_axis=0, concat_axis=2,...  53.8 us
    all_gather x1, waiting for transfers between devices, on_device(): lax.all_gather(down_weight, 'dp', axis=1, tiled=True)  32.8 us
    reduce_scatter x1, waiting for transfers between devices, on_device(): lax.psum_scatter(per_token.astype(jnp.bfloat16), 'tensor', scatter_dimens...  20.7 us
    all_to_all x1, waiting for transfers between devices, on_device(): lax.all_to_all(to_buckets(cotangent), 'expert', split_axis=0, concat_axis...  20.1 us
    all_to_all x1, starting transfers between devices, on_device(): lax.all_to_all(to_buckets(tokens), 'expert', split_axis=0, concat_axis=2,...  15.6 us
    all_gather x1, waiting for transfers between devices, on_device(): lax.all_gather(up_weight, 'dp', axis=1, tiled=True)  13.1 us
    all_to_all x1, starting transfers between devices, on_device(): lax.all_to_all(outgoing_back, 'expert', split_axis=2, concat_axis=0, tile...  12.6 us
  transfers between devices with their start and end apart: 9, of which 6 were waited for; matrix products, arithmetic and copies ran while one was open for 10% of the time, Pallas kernels for 0%

commit v1 on v0

--- a/solution.py
+++ b/solution.py
@@ -4,6 +4,19 @@
 from jax.sharding import PartitionSpec as P
 
 CAP = 8
+
+
+def collect(array, axis, dim):
+    ways = lax.axis_size(axis)
+    up = [(d, (d + 1) % ways) for d in range(ways)]
+    down = [(d, (d - 1) % ways) for d in range(ways)]
+    earlier, later = ([array], [array])
+    for _ in range(ways // 2):
+        earlier.append(lax.ppermute(earlier[-1], axis, up))
+    for _ in range((ways - 1) // 2):
+        later.append(lax.ppermute(later[-1], axis, down))
+    line = jnp.concatenate([*earlier[::-1], *later[1:]], axis=dim)
+    return jnp.roll(line, (lax.axis_index(axis) - ways // 2) * array.shape[dim], axis=dim)
 
 
 def bucket_matrix(expert_ids, expert_count, capacity):
@@ -27,7 +40,7 @@
     gate_full, up_full, down_full = (
         lax.all_gather(gate_weight, "dp", axis=1, tiled=True),
         lax.all_gather(up_weight, "dp", axis=1, tiled=True),
-        lax.all_gather(down_weight, "dp", axis=1, tiled=True),
+        collect(down_weight, "dp", 1),
     )
 
     def to_buckets(rows):

time: 282 us -> 286 us (1.014)
  waiting for transfers between devices: 197 us -> 186 us
  starting transfers between devices: 32.5 us -> 42.4 us
  local copies, waits for them, and re-layouts: 9.44 us -> 16 us
    all_gather x1 -> x0, waiting for transfers between devices: 32.8 us -> none  [on_device(): lax.all_gather(down_weight, 'dp', axis=1, tiled=True)]
    ppermute x0 -> x3, waiting for transfers between devices: none -> 20.6 us  [the longest x2 17 us: collect(): earlier.append(lax.ppermute(earlier[-1], axis, up))]
    ppermute x0 -> x3, starting transfers between devices: none -> 9.5 us  [the longest x2 6.96 us: collect(): earlier.append(lax.ppermute(earlier[-1], axis, up))]
    unnamed x11 -> x20, local copies, waits for them, and re-layouts: 6.51 us -> 12.2 us
    all_to_all x1, waiting for transfers between devices: 20.1 us -> 14.5 us  [on_device(): lax.all_to_all(to_buckets(cotangent), 'expert', split_axis=0, concat_axis...]
    all_gather x1, waiting for transfers between devices: 13.1 us -> 17.8 us  [on_device(): lax.all_gather(up_weight, 'dp', axis=1, tiled=True)]
  transfers between devices with their start and end apart: 9 -> 11, of which waited for: 6 -> 9; matrix products, arithmetic and copies ran while one was open for 10% -> 12% of each run, Pallas kernels for 0% -> 0%
where the time goes in v1:
time: 286 us; the launch traced here: 285 us
  waiting for transfers between devices  186 us (65%)
  starting transfers between devices  42.4 us (15%)
  matrix products  16.9 us (6%)
  local copies, waits for them, and re-layouts  16 us (6%)
  between operations  14 us (5%)
  other arithmetic  10.5 us (4%)
    all_to_all x1, waiting for transfers between devices, on_device(): lax.all_to_all(to_buckets(tokens), 'expert', split_axis=0, concat_axis=2,...  54.5 us
    all_to_all x1, waiting for transfers between devices, on_device(): lax.all_to_all(outgoing_back, 'expert', split_axis=2, concat_axis=0, tile...  54.2 us
    reduce_scatter x1, waiting for transfers between devices, on_device(): lax.psum_scatter(per_token.astype(jnp.bfloat16), 'tensor', scatter_dimens...  20.8 us
    all_gather x1, waiting for transfers between devices, on_device(): lax.all_gather(up_weight, 'dp', axis=1, tiled=True)  17.8 us
    ppermute x2, waiting for transfers between devices, collect(): earlier.append(lax.ppermute(earlier[-1], axis, up))  17 us
    all_to_all x1, starting transfers between devices, on_device(): lax.all_to_all(to_buckets(tokens), 'expert', split_axis=0, concat_axis=2,...  15.5 us
    all_to_all x1, waiting for transfers between devices, on_device(): lax.all_to_all(to_buckets(cotangent), 'expert', split_axis=0, concat_axis...  14.5 us
    all_to_all x1, starting transfers between devices, on_device(): lax.all_to_all(outgoing_back, 'expert', split_axis=2, concat_axis=0, tile...  12.6 us
  transfers between devices with their start and end apart: 11, of which 9 were waited for; matrix products, arithmetic and copies ran while one was open for 12% of the time, Pallas kernels for 0%

profile of v1, /device:TPU:8, one launch (start us, length us, event | category | flops | bytes accessed | tf_op | source)
XLA Modules:
  0.0 285.5 jit_solution(13614179883614619765)
XLA Ops:
  11.1 15.5 %all-to-all-start.1 = ((bf16[32,1,8,2048]{3,2,1,0:T(8,128)(2,1)}), bf16[32,1,8,2048]{3,2,1,0:T(8,128)(2,1)S(1)}, u32[]{:S(2)}, u32[]{:S(2)}) async-start(bf16[32,1,8,2048]{3,2,1,0:T(8,128)(2,1)} %fusion.5), calls=%async_computation.1 | async-start | bytes 2097152 | tf_op jit(solution)/shard_map/all_to_all | solution.py:51
  28.0 54.5 %all-to-all-done.1 = bf16[32,1,8,2048]{3,2,1,0:T(8,128)(2,1)S(1)} async-done(((bf16[32,1,8,2048]{3,2,1,0:T(8,128)(2,1)}), bf16[32,1,8,2048]{3,2,1,0:T(8,128)(2,1)S(1)}, u32[]{:S(2)}, u32[]{:S(2)}) %all-to-all-start.1) | async-done | bytes 1048608 | tf_op jit(solution)/shard_map/all_to_all | solution.py:51
  82.6 4.7 %all-to-all-start = ((bf16[32,1,8,2048]{3,2,1,0:T(8,128)(2,1)}), bf16[32,1,8,2048]{3,2,1,0:T(8,128)(2,1)}, u32[]{:S(2)}, u32[]{:S(2)}) async-start(bf16[32,1,8,2048]{3,2,1,0:T(8,128)(2,1)} %fusion.4), calls=%async_computation | async-start | bytes 2097152 | tf_op jit(solution)/shard_map/all_to_all | solution.py:52
  88.0 3.5 %collective-permute-start = (bf16[1,512,352]{1,2,0:T(8,128)(2,1)S(1)}, bf16[1,512,352]{1,2,0:T(8,128)(2,1)S(1)}, u32[]{:S(2)}, u32[]{:S(2)}) collective-permute-start(bf16[1,512,352]{1,2,0:T(8,128)(2,1)S(1)} %copy-done.2), channel_id=1, source_target_pairs={{0,128},{128,256},{256,384},{384,0},{1,129},{129,257},{257,385},{3... | collective-permute-start | bytes 1081352 | tf_op jit(solution)/shard_map/ppermute | solution.py:15
  91.6 8.7 %collective-permute-done = bf16[1,512,352]{1,2,0:T(8,128)(2,1)S(1)} collective-permute-done((bf16[1,512,352]{1,2,0:T(8,128)(2,1)S(1)}, bf16[1,512,352]{1,2,0:T(8,128)(2,1)S(1)}, u32[]{:S(2)}, u32[]{:S(2)}) %collective-permute-start) | collective-permute-done | bytes 360480 | tf_op jit(solution)/shard_map/ppermute | solution.py:15
  100.3 3.5 %collective-permute-start.1 = (bf16[1,512,352]{1,2,0:T(8,128)(2,1)S(1)}, bf16[1,512,352]{1,2,0:T(8,128)(2,1)S(1)}, u32[]{:S(2)}, u32[]{:S(2)}) collective-permute-start(bf16[1,512,352]{1,2,0:T(8,128)(2,1)S(1)} %collective-permute-done), channel_id=1, source_target_pairs={{0,128},{128,256},{256,384},{384,0},{1,129},{129,257},{257,385},{3... | collective-permute-start | bytes 1081352 | tf_op jit(solution)/shard_map/ppermute | solution.py:15
  103.8 2.5 collective-permute-start.2
  106.4 8.3 %collective-permute-done.1 = bf16[1,512,352]{1,2,0:T(8,128)(2,1)S(1)} collective-permute-done((bf16[1,512,352]{1,2,0:T(8,128)(2,1)S(1)}, bf16[1,512,352]{1,2,0:T(8,128)(2,1)S(1)}, u32[]{:S(2)}, u32[]{:S(2)}) %collective-permute-start.1) | collective-permute-done | bytes 360480 | tf_op jit(solution)/shard_map/ppermute | solution.py:15
  117.2 3.5 %collective-permute-done.2 = bf16[1,512,352]{1,2,0:T(8,128)(2,1)S(1)} collective-permute-done((bf16[1,512,352]{1,2,0:T(8,128)(2,1)S(1)}, bf16[1,512,352]{1,2,0:T(8,128)(2,1)S(1)}, u32[]{:S(2)}, u32[]{:S(2)}) %collective-permute-start.2) | collective-permute-done | bytes 360480 | tf_op jit(solution)/shard_map/ppermute | solution.py:17
  124.7 2.6 all-gather.5.cloned.1.call-done
  127.3 1.9 fusion.8
  129.3 14.5 %all-to-all-done = bf16[32,1,8,2048]{3,2,1,0:T(8,128)(2,1)} async-done(((bf16[32,1,8,2048]{3,2,1,0:T(8,128)(2,1)}), bf16[32,1,8,2048]{3,2,1,0:T(8,128)(2,1)}, u32[]{:S(2)}, u32[]{:S(2)}) %all-to-all-start) | async-done | bytes 1048608 | tf_op jit(solution)/shard_map/all_to_all | solution.py:52
  143.7 2.3 multiply_convert_fusion
  146.0 17.8 %all-gather.3.cloned.1.call-done = bf16[1,2048,352]{1,2,0:T(8,128)(2,1)} async-done(((bf16[1,512,352]{1,2,0:T(8,128)(2,1)}), bf16[1,2048,352]{1,2,0:T(8,128)(2,1)}) %all-gather.3.cloned.1.call-update) | async-done | bytes 1441808 | tf_op jit(solution)/shard_map/all_gather | solution.py:42
  163.7 1.9 fusion.25
  165.7 1.7 fusion.1
  169.5 2.9 %copy.21 = bf16[1,1,256,2048]{3,1,0,2:T(2,128)(2,1)} copy(bf16[1,1,256,2048]{3,2,1,0:T(8,128)(2,1)S(1)} %fusion.3) | data formatting | bytes 2097152 | tf_op jit(solution)/shard_map/reshape | solution.py:83
  173.0 8.0 %reduce = bf16[256,2048]{1,0:T(8,128)(2,1)S(1)} reduce(bf16[256,1,1,2048]{3,2,1,0:T(2,128)(2,1)} %bitcast.66, bf16[]{:T(256)} %broadcast.20), dimensions={1,2}, to_apply=%bitcast.65.reduce_sub_computation | reduce | bytes 2097154
  181.0 1.9 reshape.108
  182.9 12.6 %all-to-all-start.2 = ((bf16[32,2,8192]{2,1,0:T(2,128)(2,1)}), bf16[32,2,8192]{2,1,0:T(2,128)(2,1)S(1)}, u32[]{:S(2)}, u32[]{:S(2)}) async-start(bf16[32,2,8192]{2,1,0:T(2,128)(2,1)} %reshape.108), calls=%async_computation.2 | async-start | bytes 2097152 | tf_op jit(solution)/shard_map/all_to_all | solution.py:86
  197.3 54.2 %all-to-all-done.2 = bf16[32,2,8192]{2,1,0:T(2,128)(2,1)S(1)} async-done(((bf16[32,2,8192]{2,1,0:T(2,128)(2,1)}), bf16[32,2,8192]{2,1,0:T(2,128)(2,1)S(1)}, u32[]{:S(2)}, u32[]{:S(2)}) %all-to-all-start.2) | async-done | bytes 1048608 | tf_op jit(solution)/shard_map/all_to_all | solution.py:86
  251.5 3.5 %reshape.109 = bf16[256,1,1,2048]{3,2,1,0:T(2,128)(2,1)} reshape(bf16[32,2,8192]{2,1,0:T(2,128)(2,1)S(1)} %all-to-all-done.2) | data formatting | bytes 2097152
  255.0 3.1 %convolution_convert_fusion.4 = bf16[128,2048]{1,0:T(8,128)(2,1)} fusion(bf16[1,1,256,2048]{3,1,0,2:T(2,128)(2,1)} %bitcast.67, s32[128]{0:T(128)S(1)} %multiply_add_fusion), kind=kOutput, calls=%fused_computation.11 | convolution fusion | flops 134512640 | bytes 1573376 | tf_op jit(solution)/shard_map/dot_general | solution.py:88
  258.2 20.8 %reduce-scatter.4.cloned.1.call-done = bf16[128,512]{1,0:T(8,128)(2,1)} async-done(((bf16[128,2048]{1,0:T(8,128)(2,1)}), bf16[128,512]{1,0:T(8,128)(2,1)}) %reduce-scatter.4.cloned.1.call-update) | async-done | bytes 131088 | tf_op jit(solution)/shard_map/reduce_scatter | solution.py:89
  (40 shorter events, 17.1 us)
Async XLA Ops:
  7.2 2.5 copy-start
  7.2 19.4 %copy-start.4 = (bf16[128,2048]{1,0:T(8,128)(2,1)S(1)}, bf16[128,2048]{1,0:T(8,128)(2,1)}, u32[]{:S(2)}) copy-start(bf16[128,2048]{1,0:T(8,128)(2,1)} %param.7) | copy-start | bytes 1572868
  11.1 71.5 %all-to-all-start.1 = ((bf16[32,1,8,2048]{3,2,1,0:T(8,128)(2,1)}), bf16[32,1,8,2048]{3,2,1,0:T(8,128)(2,1)S(1)}, u32[]{:S(2)}, u32[]{:S(2)}) async-start(bf16[32,1,8,2048]{3,2,1,0:T(8,128)(2,1)} %fusion.5), calls=%async_computation.1 | async-start | bytes 2097152 | tf_op jit(solution)/shard_map/all_to_all | solution.py:51
  26.6 61.4 %copy-start.2 = (bf16[1,512,352]{1,2,0:T(8,128)(2,1)S(1)}, bf16[1,512,352]{1,2,0:T(8,128)(2,1)}, u32[]{:S(2)}) copy-start(bf16[1,512,352]{1,2,0:T(8,128)(2,1)} %param.11) | copy-start | bytes 1081348
  82.6 61.2 %all-to-all-start = ((bf16[32,1,8,2048]{3,2,1,0:T(8,128)(2,1)}), bf16[32,1,8,2048]{3,2,1,0:T(8,128)(2,1)}, u32[]{:S(2)}, u32[]{:S(2)}) async-start(bf16[32,1,8,2048]{3,2,1,0:T(8,128)(2,1)} %fusion.4), calls=%async_computation | async-start | bytes 2097152 | tf_op jit(solution)/shard_map/all_to_all | solution.py:52
  87.2 40.1 %all-gather.5.cloned.1.call-start = ((), (), s32[]{:S(2)}) async-start(), calls=%async_computation.7 | async-start | bytes 1802240 | tf_op jit(solution)/shard_map/all_gather | solution.py:41
  88.0 75.8 %all-gather.3.cloned.1.call-start = ((), (), s32[]{:S(2)}) async-start(), calls=%async_computation.6 | async-start | bytes 1802240 | tf_op jit(solution)/shard_map/all_gather | solution.py:42
  88.0 12.3 %collective-permute-start = (bf16[1,512,352]{1,2,0:T(8,128)(2,1)S(1)}, bf16[1,512,352]{1,2,0:T(8,128)(2,1)S(1)}, u32[]{:S(2)}, u32[]{:S(2)}) collective-permute-start(bf16[1,512,352]{1,2,0:T(8,128)(2,1)S(1)} %copy-done.2), channel_id=1, source_target_pairs={{0,128},{128,256},{256,384},{384,0},{1,129},{129,257},{257,385},{3... | collective-permute-start | bytes 1081352 | tf_op jit(solution)/shard_map/ppermute | solution.py:15
  91.6 166.6 %reduce-scatter.6.cloned.1.call-start = ((), (), s32[]{:S(2)}) async-start(), calls=%async_computation.9 | async-start | bytes 1802240 | tf_op jit(solution)/shard_map/reduce_scatter | solution.py:75
  100.3 14.4 %collective-permute-start.1 = (bf16[1,512,352]{1,2,0:T(8,128)(2,1)S(1)}, bf16[1,512,352]{1,2,0:T(8,128)(2,1)S(1)}, u32[]{:S(2)}, u32[]{:S(2)}) collective-permute-start(bf16[1,512,352]{1,2,0:T(8,128)(2,1)S(1)} %collective-permute-done), channel_id=1, source_target_pairs={{0,128},{128,256},{256,384},{384,0},{1,129},{129,257},{257,385},{3... | collective-permute-start | bytes 1081352 | tf_op jit(solution)/shard_map/ppermute | solution.py:15
  103.8 16.9 %collective-permute-start.2 = (bf16[1,512,352]{1,2,0:T(8,128)(2,1)S(1)}, bf16[1,512,352]{1,2,0:T(8,128)(2,1)S(1)}, u32[]{:S(2)}, u32[]{:S(2)}) collective-permute-start(bf16[1,512,352]{1,2,0:T(8,128)(2,1)S(1)} %copy-done.2), channel_id=1, source_target_pairs={{0,384},{128,0},{256,128},{384,256},{1,385},{129,1},{257,129},{385... | collective-permute-start | bytes 1081352 | tf_op jit(solution)/shard_map/ppermute | solution.py:17
  165.7 1.7 copy-start.1
  167.4 1.4 copy-start.3
  182.9 68.6 %all-to-all-start.2 = ((bf16[32,2,8192]{2,1,0:T(2,128)(2,1)}), bf16[32,2,8192]{2,1,0:T(2,128)(2,1)S(1)}, u32[]{:S(2)}, u32[]{:S(2)}) async-start(bf16[32,2,8192]{2,1,0:T(2,128)(2,1)} %reshape.108), calls=%async_computation.2 | async-start | bytes 2097152 | tf_op jit(solution)/shard_map/all_to_all | solution.py:86
  195.5 62.7 %reduce-scatter.8.cloned.1.call-start = ((), (), s32[]{:S(2)}) async-start(), calls=%async_computation.10 | async-start | bytes 1802240 | tf_op jit(solution)/shard_map/reduce_scatter | solution.py:78
  197.2 81.7 %reduce-scatter.4.cloned.1.call-start = ((), (), s32[]{:S(2)}) async-start(), calls=%async_computation.8 | async-start | bytes 655360 | tf_op jit(solution)/shard_map/reduce_scatter | solution.py:89
Sparse Core Ops, SparseCore 0:
  90.2 37.0 all-gather.4
  129.4 34.2 all-gather.2
  167.5 32.7 reduce-scatter.5
  203.6 32.5 reduce-scatter.7
  258.3 20.6 reduce-scatter.3
